TPU v7x, 128 devices: a whole 4x4x4 slice. The times are simulated.
128 devices in a mesh: seq: 16 (over x_lo, z, core), fsdp: 8 (over x_hi, y).
Axes of the slice: x: 4 (x_hi: 2, x_lo: 2; x = x_hi * 2 + x_lo), y: 4, z: 4, core: 2. Of those that a mesh axis runs over, the one named last changes fastest.
Arguments:
- queries: bfloat16 [8, 4096, 4096], P('fsdp', 'seq'), may hold values from -60 to 60
- keys: bfloat16 [8, 4096, 4096], P('fsdp', 'seq'), may hold values from -4.8 to 4.8
- values: bfloat16 [8, 4096, 4096], P('fsdp', 'seq'), may hold values from -6 to 6
- out_weight: bfloat16 [4096, 3072], P(('seq', 'fsdp')), may hold values from -0.75 to 0.75
- block_lists: int32 [8, 32, 32, 8], P('fsdp'), may hold values from 0 to 31, as said below
- block_counts: int32 [8, 32, 32], P('fsdp'), may hold values from 1 to 8, as said below
Outputs:
- projected: bfloat16 [8, 4096, 3072], P('fsdp', 'seq')
Inputs may be any that keep to these rules, and one draw needn't show every extreme that they name: `block_lists`: entry j = 0 of every list is the query block itself; the 8 entries of a list are distinct blocks; entries at slots j >= block_counts are ignored. `block_counts`: in every sequence some head and query block has 8 live slots.
All inputs are finite; a program needn't handle non-finite values.
Results may differ from a plain program's by a relative error of at most 0.0085.
Values may be sent and summed in bfloat16 or wider, within the bound.
A program may use at most 128 MiB of HBM per device.

v0:
```python
import jax
import jax.numpy as jnp
from jax import lax
from jax.sharding import PartitionSpec as P


def attend_head(query_rows, key_rows, value_rows, block_ids, live_counts):
    block_total = live_counts.shape[0]
    head_width = query_rows.shape[1]
    block_size = query_rows.shape[0] // block_total
    query_blocks = query_rows.reshape(block_total, block_size, head_width)
    key_blocks = key_rows.reshape(block_total, block_size, head_width)
    value_blocks = value_rows.reshape(block_total, block_size, head_width)
    factor = head_width ** (-0.5)

    def advance(column, carry):
        running, denom_sum, accumulated = carry
        picked = block_ids[:, column]
        key_tile = key_blocks[picked]
        value_tile = value_blocks[picked]
        scores = (
            jnp.einsum("qpd,qkd->qpk", query_blocks, key_tile, preferred_element_type=jnp.float32)
            * factor
        )
        usable = (column < live_counts)[:, None, None]
        scores = jnp.where(usable, scores, -jnp.inf)
        updated = jnp.maximum(running, jnp.max(scores, axis=2))
        rescale = jnp.exp(running - updated)
        weights = jnp.exp(scores - updated[:, :, None])
        denom_sum = denom_sum * rescale + jnp.sum(weights, axis=2)
        accumulated = accumulated * rescale[:, :, None] + jnp.einsum(
            "qpk,qkd->qpd",
            weights.astype(jnp.bfloat16),
            value_tile,
            preferred_element_type=jnp.float32,
        )
        return (updated, denom_sum, accumulated)

    initial = (
        jnp.full((block_total, block_size), -jnp.inf, jnp.float32),
        jnp.zeros((block_total, block_size), jnp.float32),
        jnp.zeros((block_total, block_size, head_width), jnp.float32),
    )
    trip_count = jnp.max(live_counts)
    running, denom_sum, accumulated = lax.fori_loop(0, trip_count, advance, initial)
    return (accumulated / denom_sum[:, :, None]).astype(jnp.bfloat16).reshape(-1, head_width)


def shards(queries, keys, values, out_weight, block_lists, block_counts):
    groups = lax.axis_size("seq")
    rank_here = lax.axis_index("seq")
    head_count = block_counts.shape[1]
    head_width = queries.shape[2] // head_count
    heads_here = head_count // groups
    local_query = queries[0]
    local_key = keys[0]
    local_value = values[0]
    lists_here = block_lists[0]
    counts_here = block_counts[0]
    chosen = jnp.arange(head_count, dtype=jnp.int32)
    head_query, head_key, head_value = (
        lax.all_to_all(local_query, "seq", split_axis=1, concat_axis=0, tiled=True),
        lax.all_to_all(local_key, "seq", split_axis=1, concat_axis=0, tiled=True),
        lax.all_to_all(local_value, "seq", split_axis=1, concat_axis=0, tiled=True),
    )
    mine = lax.dynamic_slice_in_dim(chosen, rank_here * heads_here, heads_here)
    my_lists = jnp.take(lists_here, mine, axis=0)
    my_counts = jnp.take(counts_here, mine, axis=0)
    outputs = []
    for member in range(heads_here):
        lower = member * head_width
        upper = lower + head_width
        outputs.append(
            attend_head(
                head_query[:, lower:upper],
                head_key[:, lower:upper],
                head_value[:, lower:upper],
                my_lists[member],
                my_counts[member],
            )
        )
    attended = jnp.concatenate(outputs, axis=1)
    returned = lax.all_to_all(attended, "seq", split_axis=0, concat_axis=1, tiled=True)
    result = jnp.dot(
        returned,
        lax.all_gather(out_weight, ("seq", "fsdp"), axis=0, tiled=True),
        preferred_element_type=jnp.float32,
    )
    return result.astype(jnp.bfloat16)[None]


def solution(mesh):
    return jax.shard_map(
        shards,
        mesh=mesh,
        in_specs=(
            P("fsdp", "seq", None),
            P("fsdp", "seq", None),
            P("fsdp", "seq", None),
            P(("seq", "fsdp"), None),
            P("fsdp", None, None, None),
            P("fsdp", None, None),
        ),
        out_specs=P("fsdp", "seq", None),
        check_vma=False,
    )
```

profile of v0, /device:TPU:1, one launch (start us, length us, event | category | flops | bytes accessed | tf_op | source)
XLA Modules:
  0.0 440.1 jit_solution(16253990267266761584)
XLA Ops:
  7.3 3.3 copy.28
  10.5 2.4 copy.29
  13.0 7.8 %all-to-all-start = ((bf16[256,16,256]{2,0,1:T(8,128)(2,1)}), bf16[256,16,256]{2,0,1:T(8,128)(2,1)S(1)}, u32[]{:S(2)}, u32[]{:S(2)}) async-start(bf16[256,16,256]{2,0,1:T(8,128)(2,1)} %copy.29), calls=%async_computation | async-start | bytes 4194304 | tf_op jit(solution)/shard_map/all_to_all | solution.py:63
  20.7 4.1 copy.30
  24.8 3.9 copy.31
  28.7 28.7 %all-to-all-done = bf16[256,16,256]{2,0,1:T(8,128)(2,1)S(1)} async-done(((bf16[256,16,256]{2,0,1:T(8,128)(2,1)}), bf16[256,16,256]{2,0,1:T(8,128)(2,1)S(1)}, u32[]{:S(2)}, u32[]{:S(2)}) %all-to-all-start) | async-done | bytes 2097184 | tf_op jit(solution)/shard_map/all_to_all | solution.py:63
  57.5 4.8 %all-to-all-start.1 = ((bf16[256,16,256]{2,0,1:T(8,128)(2,1)}), bf16[256,16,256]{2,0,1:T(8,128)(2,1)}, u32[]{:S(2)}, u32[]{:S(2)}) async-start(bf16[256,16,256]{2,0,1:T(8,128)(2,1)} %copy.31), calls=%async_computation.1 | async-start | bytes 4194304 | tf_op jit(solution)/shard_map/all_to_all | solution.py:62
  63.5 4.1 copy.32
  67.6 3.9 copy.33
  71.7 26.1 %all-to-all-done.1 = bf16[256,16,256]{2,0,1:T(8,128)(2,1)} async-done(((bf16[256,16,256]{2,0,1:T(8,128)(2,1)}), bf16[256,16,256]{2,0,1:T(8,128)(2,1)}, u32[]{:S(2)}, u32[]{:S(2)}) %all-to-all-start.1) | async-done | bytes 2097184 | tf_op jit(solution)/shard_map/all_to_all | solution.py:62
  97.8 4.7 %all-to-all-start.2 = ((bf16[256,16,256]{2,0,1:T(8,128)(2,1)}), bf16[256,16,256]{2,0,1:T(8,128)(2,1)}, u32[]{:S(2)}, u32[]{:S(2)}) async-start(bf16[256,16,256]{2,0,1:T(8,128)(2,1)} %copy.33), calls=%async_computation.2 | async-start | bytes 4194304 | tf_op jit(solution)/shard_map/all_to_all | solution.py:64
  104.7 3.0 fusion.24
  107.7 30.0 %all-to-all-done.2 = bf16[256,16,256]{2,0,1:T(8,128)(2,1)} async-done(((bf16[256,16,256]{2,0,1:T(8,128)(2,1)}), bf16[256,16,256]{2,0,1:T(8,128)(2,1)}, u32[]{:S(2)}, u32[]{:S(2)}) %all-to-all-start.2) | async-done | bytes 2097184 | tf_op jit(solution)/shard_map/all_to_all | solution.py:64
  137.6 3.1 fusion.23
  142.3 87.4 %while.28 = (s32[]{:T(128)}, f32[32,128]{1,0:T(8,128)S(1)}, f32[32,128]{1,0:T(8,128)S(1)}, f32[32,128,128]{2,1,0:T(8,128)}, s32[]{:T(128)}, /*index=5*/s32[32]{0...) while((s32[]{:T(128)}, f32[32,128]{1,0:T(8,128)S(1)}, ...), condition=%wide.region_4.5_spmd, body=%wide.region_1.0_spmd.sunk | while | flops 275260544 | bytes 18093096 | solution.py:45
  149.6 3.6 multiply_add_fusion.9
  160.4 3.6 multiply_add_fusion.9
  166.7 2.1 bitcast_reduce_fusion.4
  171.3 3.6 multiply_add_fusion.9
  182.2 3.5 multiply_add_fusion.9
  193.0 3.6 multiply_add_fusion.9
  203.8 3.5 multiply_add_fusion.9
  214.7 3.6 multiply_add_fusion.9
  225.5 3.5 multiply_add_fusion.9
  229.7 2.8 divide_convert_fusion.1
  234.0 22.2 %while.29 = (s32[]{:T(128)}, f32[32,128]{1,0:T(8,128)S(1)}, f32[32,128]{1,0:T(8,128)S(1)}, f32[32,128,128]{2,1,0:T(8,128)}, s32[]{:T(128)}, /*index=5*/s32[32]{0...) while((s32[]{:T(128)}, f32[32,128]{1,0:T(8,128)S(1)}, ...), condition=%wide.region_9.10_spmd, body=%wide.region_6.9_spmd.sunk | while | flops 275260544 | bytes 18093096 | solution.py:45
  241.3 3.6 multiply_add_fusion.11
  252.1 3.6 multiply_add_fusion.11
  258.6 87.6 %all_to_all.73 = bf16[16,256,256]{2,1,0:T(8,128)(2,1)} all-to-all(bf16[16,256,256]{2,1,0:T(8,128)(2,1)S(1)} %pad_maximum_fusion), channel_id=1, replica_groups=mesh['seq'=16,'fsdp'=8] {'seq'}, dimensions={0} | all-to-all | bytes 4194304 | tf_op jit(solution)/shard_map/all_to_all | solution.py:83
  346.2 2.8 copy.34
  349.0 71.2 %all-gather.2.cloned.1.call-done = bf16[4096,3072]{1,0:T(8,128)(2,1)} async-done(((bf16[32,3072]{1,0:T(8,128)(2,1)}), bf16[4096,3072]{1,0:T(8,128)(2,1)}) %all-gather.2.cloned.1.call-update) | async-done | bytes 25165840 | tf_op jit(solution)/shard_map/all_gather | solution.py:86
  420.3 13.0 %fusion.22 = bf16[1,256,3072]{2,1,0:T(8,128)(2,1)} fusion(bf16[256,4096]{0,1:T(8,128)(2,1)S(1)} %bitcast.99, bf16[4096,3072]{1,0:T(8,128)(2,1)} %all-gather.2.cloned.1.call-done), kind=kOutput, calls=%fused_computation.45 | convolution fusion | flops 6443237376 | bytes 28835840 | tf_op jit(solution)/shard_map/dot_general | solution.py:84
  (127 shorter events, 73.7 us)
Async XLA Ops:
  6.5 56.4 %copy-start = (s32[1,32,32,8]{2,3,1,0:T(8,128)S(1)}, s32[1,32,32,8]{2,3,1,0:T(8,128)}, u32[]{:S(2)}) copy-start(s32[1,32,32,8]{2,3,1,0:T(8,128)} %param.14) | copy-start | bytes 98308
  6.5 413.7 %all-gather.2.cloned.1.call-start = ((), (), s32[]{:S(2)}) async-start(), calls=%async_computation.4 | async-start | bytes 25362432 | tf_op jit(solution)/shard_map/all_gather | solution.py:86
  13.0 44.5 %all-to-all-start = ((bf16[256,16,256]{2,0,1:T(8,128)(2,1)}), bf16[256,16,256]{2,0,1:T(8,128)(2,1)S(1)}, u32[]{:S(2)}, u32[]{:S(2)}) async-start(bf16[256,16,256]{2,0,1:T(8,128)(2,1)} %copy.29), calls=%async_computation | async-start | bytes 4194304 | tf_op jit(solution)/shard_map/all_to_all | solution.py:63
  28.7 33.7 %copy-start.3 = (s32[1,32,32]{2,1,0:T(8,128)S(1)}, s32[1,32,32]{2,1,0:T(8,128)}, u32[]{:S(2)}) copy-start(s32[1,32,32]{2,1,0:T(8,128)} %param.15) | copy-start | bytes 12292
  57.5 40.3 %all-to-all-start.1 = ((bf16[256,16,256]{2,0,1:T(8,128)(2,1)}), bf16[256,16,256]{2,0,1:T(8,128)(2,1)}, u32[]{:S(2)}, u32[]{:S(2)}) async-start(bf16[256,16,256]{2,0,1:T(8,128)(2,1)} %copy.31), calls=%async_computation.1 | async-start | bytes 4194304 | tf_op jit(solution)/shard_map/all_to_all | solution.py:62
  97.8 39.9 %all-to-all-start.2 = ((bf16[256,16,256]{2,0,1:T(8,128)(2,1)}), bf16[256,16,256]{2,0,1:T(8,128)(2,1)}, u32[]{:S(2)}, u32[]{:S(2)}) async-start(bf16[256,16,256]{2,0,1:T(8,128)(2,1)} %copy.33), calls=%async_computation.2 | async-start | bytes 4194304 | tf_op jit(solution)/shard_map/all_to_all | solution.py:64
  256.2 2.1 copy-start.2
  420.3 13.0 %copy-start.1 = (s32[1,32,32,8]{2,3,1,0:T(8,128)S(1)}, s32[1,32,32,8]{2,3,1,0:T(8,128)}, u32[]{:S(2)}) copy-start(s32[1,32,32,8]{2,3,1,0:T(8,128)} %param.14) | copy-start | bytes 98308
Sparse Core Ops, SparseCore 0:
  9.1 411.1 all-gather.1
where the time goes:
time: 445 us; the launch traced here: 440 us
  waiting for transfers between devices  157 us (35%)
  blocking collectives  87.6 us (20%)
  local copies, waits for them, and re-layouts  76 us (17%)
  matrix products  69.4 us (16%)
  starting transfers between devices  17.3 us (4%)
  between operations  13.5 us (3%)
  other arithmetic  11.5 us (3%)
  loops' own time  7.99 us (2%)
    all_to_all x1, blocking collectives, shards(): lax.all_to_all(attended, 'seq', split_axis=0, concat_axis=1, tiled=True)  87.6 us
    all_gather x1, waiting for transfers between devices, shards(): lax.all_gather(out_weight, ('seq', 'fsdp'), axis=0, tiled=True)  71.2 us
    dot_general x10, matrix products, advance(): jnp.einsum('qpk,qkd->qpd', weights.astype(jnp.bfloat16), value_tile, pref...  35.6 us
    all_to_all x1, waiting for transfers between devices, shards(): lax.all_to_all(local_value, 'seq', split_axis=1, concat_axis=0, tiled=True)  30 us
    all_to_all x1, waiting for transfers between devices, shards(): lax.all_to_all(local_key, 'seq', split_axis=1, concat_axis=0, tiled=True)  28.7 us
    all_to_all x1, waiting for transfers between devices, shards(): lax.all_to_all(local_query, 'seq', split_axis=1, concat_axis=0, tiled=True)  26.1 us
    dot_general x10, matrix products, advance(): jnp.einsum('qpd,qkd->qpk', query_blocks, key_tile, preferred_element_type...  20.9 us
    gather x10, local copies, waits for them, and re-layouts, advance(): key_tile = key_blocks[picked]  19.8 us
  transfers between devices with their start and end apart: 4, of which 4 were waited for; matrix products, arithmetic and copies ran while one was open for 33% of the time, Pallas kernels for 0%

commit v1 on v0

v1 whole, which is shorter than its diff:
```python
import functools
import math

import jax
import jax.numpy as jnp
from jax import lax
from jax.experimental import pallas as pl
from jax.experimental.pallas import tpu as pltpu
from jax.sharding import PartitionSpec as P

MESH = pl.DeviceIdType.MESH
PARTS = dict(a2a=True, gather=True, attend=True, project=True)


def kernel(
    lists, counts, q_hbm, k_hbm, v_hbm, w_hbm, out_hbm,
    q0, q1, k0, k1, v0, v1, sent, rows, wb, outv,
    in_sems, out_sems, own_sem, w_recv, w_send, sib_recv, sib_send,
    back_recv, back_send,
):
    seq = lax.axis_index("seq")
    fs = lax.axis_index("fsdp")
    xl, z, c = seq // 8, (seq // 2) % 4, seq % 2
    xh, y = fs // 4, fs % 4
    qb, kb, vb = (q0, q1), (k0, k1), (v0, v1)
    heads, blocks, dim = len(qb), q0.shape[0], q0.shape[2]
    span = q_hbm.shape[1]
    per = span // q0.shape[1]

    def seq_of(a, b, d):
        return (a * 4 + b) * 2 + d

    up, down = xh * 4 + (y + 1) % 4, xh * 4 + (y + 3) % 4
    opp = xh * 4 + (y + 2) % 4
    far = (1 - xh) * 4
    x_peer = (seq_of(1 - xl, z, c), fs)
    far_peer = (seq_of(1 - xl, z, c), far + y)
    sibling = (seq_of(xl, z, 1 - c), fs)
    up_peer, down_peer = (seq, up), (seq, down)

    barrier = pltpu.get_barrier_semaphore()
    for d in range(1, 16):
        pl.semaphore_signal(barrier, inc=1, device_id=((seq + d) % 16, fs), device_id_type=MESH)
    for peer in (far_peer, up_peer, down_peer):
        pl.semaphore_signal(barrier, inc=1, device_id=peer, device_id_type=MESH)
    pl.semaphore_wait(barrier, 18)

    pending = []

    def send(src, dst, ssem, rsem, peer):
        copy = pltpu.make_async_remote_copy(
            src_ref=src, dst_ref=dst, send_sem=ssem, recv_sem=rsem,
            device_id=peer, device_id_type=MESH,
        )
        copy.start()
        return copy

    def arrived(ref, sem):
        pltpu.make_async_copy(ref, ref, sem).wait()

    if PARTS["gather"]:
        own = wb.at[xl, z, c, fs]
        own_copy = pltpu.make_async_copy(w_hbm, own, own_sem.at[0])
        own_copy.start()
        for d in range(1, 4):
            pending.append(send(w_hbm, own, w_send.at[d], w_recv.at[0], (seq_of(xl, (z + d) % 4, c), fs)))

    order = [(dx, dz, dc) for dz in (2, 1, 3, 0) for dx in (1, 0) for dc in (1, 0)][:-1]

    def scatter(hbm, buf, t, h):
        for dx, dz, dc in order:
            p = seq_of((xl + dx) % 2, (z + dz) % 4, (c + dc) % 2)
            for part in range(per):
                rows_at = pl.ds(part * dim, dim)
                send(
                    hbm.at[0, rows_at, pl.ds(p * heads * dim + h * dim, dim)],
                    buf[h].at[seq * per + part],
                    out_sems.at[t, h], in_sems.at[t, h], (p, fs),
                )
        for part in range(per):
            pltpu.make_async_copy(
                hbm.at[0, pl.ds(part * dim, dim), pl.ds(seq * heads * dim + h * dim, dim)],
                buf[h].at[seq * per + part], in_sems.at[t, h],
            ).start()

    def scattered(buf, t, h):
        arrived(buf[h], in_sems.at[t, h])

    streams = ((k_hbm, kb), (q_hbm, qb), (v_hbm, vb))
    if PARTS["a2a"]:
        for t, (hbm, buf) in enumerate(streams):
            scatter(hbm, buf, t, 0)

    def piece(which, j):
        return wb.at[xl if which == 0 else 1 - xl, :, c, j]

    def to_sibling(view, n):
        pending.append(send(view, view, sib_send.at[n], sib_recv.at[n], sibling))

    def start_blocks(p):
        view = piece(p, fs)
        for kind, peer in ((0, up_peer), (1, down_peer), (2, far_peer)):
            n = 5 + p * 8 + kind
            pending.append(send(view, view, w_send.at[n], w_recv.at[2 + p * 8 + kind], peer))
        to_sibling(view, p * 8)

    def half(view, n):
        return view.at[pl.ds(2 * n, 2)]

    def relay_blocks(p):
        base = 2 + p * 8
        sbase = 5 + p * 8
        below, above = piece(p, down), piece(p, up)
        arrived(below, w_recv.at[base])
        pending.append(send(half(below, 0), half(below, 0), w_send.at[sbase + 3], w_recv.at[base + 3], up_peer))
        to_sibling(below, p * 8 + 1)
        arrived(above, w_recv.at[base + 1])
        pending.append(send(half(above, 1), half(above, 1), w_send.at[sbase + 4], w_recv.at[base + 4], down_peer))
        to_sibling(above, p * 8 + 2)
        across = piece(1 - p, far + y)
        arrived(across, w_recv.at[base + 2])
        pending.append(send(across, across, w_send.at[sbase + 5], w_recv.at[base + 5], up_peer))
        pending.append(send(across, across, w_send.at[sbase + 6], w_recv.at[base + 6], down_peer))
        to_sibling(across, p * 8 + 3)

    def last_blocks(p):
        base = 2 + p * 8
        sbase = 5 + p * 8
        facing = piece(p, opp)
        arrived(half(facing, 0), w_recv.at[base + 3])
        arrived(half(facing, 1), w_recv.at[base + 4])
        pending.append(send(facing, facing, w_send.at[sbase + 7], w_recv.at[base + 7], far_peer))
        to_sibling(facing, p * 8 + 4)

    def finish_blocks(p):
        base = 2 + p * 8
        q = 1 - p
        a, b, d = piece(q, far + (y + 3) % 4), piece(q, far + (y + 1) % 4), piece(q, far + (y + 2) % 4)
        arrived(a, w_recv.at[base + 5])
        to_sibling(a, p * 8 + 5)
        arrived(b, w_recv.at[base + 6])
        to_sibling(b, p * 8 + 6)
        arrived(d, w_recv.at[base + 7])
        to_sibling(d, p * 8 + 7)

    if PARTS["gather"]:
        own_copy.wait()
        arrived(wb.at[0, pl.ds(0, 3), c, 0], w_recv.at[0])
        pending.append(send(piece(0, fs), piece(0, fs), w_send.at[4], w_recv.at[1], x_peer))
        start_blocks(0)

    if PARTS["a2a"]:
        for t, (hbm, buf) in enumerate(streams):
            scatter(hbm, buf, t, 1)

    if PARTS["gather"]:
        arrived(piece(1, fs), w_recv.at[1])
        start_blocks(1)
        relay_blocks(0)
        last_blocks(0)

    scale = dim ** -0.5 * math.log2(math.e)

    def attend(h, i):
        base = (h * blocks + i) * 8
        live = counts[h * blocks + i]
        first = lists[base]
        q = qb[h][i]
        ids, bias = [], []
        for j in range(8):
            ids.append(jnp.where(j < live, lists[base + j], first))
            bias.append(jnp.where(j < live, 0.0, -jnp.inf).astype(jnp.float32))
        lane = lax.broadcasted_iota(jnp.int32, (1, 2 * dim), 1)
        scores = []
        for j in range(0, 8, 2):
            keys = jnp.concatenate([kb[h][ids[j]], kb[h][ids[j + 1]]], axis=0)
            scores.append(lax.dot_general(q, keys, (((1,), (1,)), ((), ())), preferred_element_type=jnp.float32))
        top = jnp.maximum(jnp.maximum(scores[0], scores[1]), jnp.maximum(scores[2], scores[3]))
        top = jnp.max(top, axis=1, keepdims=True) * scale
        total = None
        mixed = None
        for j in range(0, 8, 2):
            row = jnp.where(lane < dim, bias[j], bias[j + 1])
            weights = jnp.exp2((scores[j // 2] * scale - top) + row)
            values = jnp.concatenate([vb[h][ids[j]], vb[h][ids[j + 1]]], axis=0)
            part = jnp.dot(weights.astype(jnp.bfloat16), values, preferred_element_type=jnp.float32)
            total = weights if total is None else total + weights
            mixed = part if mixed is None else mixed + part
        total = jnp.sum(total, axis=1, keepdims=True)
        return (mixed / total).astype(jnp.bfloat16)

    def attend_head(h):
        def body(d, carry):
            p = (seq + d) % 16
            if PARTS["attend"]:
                for part in range(per):
                    sent[h, p, pl.ds(part * dim, dim), :] = attend(h, p * per + part)
            send(
                sent.at[h, p], rows.at[:, pl.ds(pl.multiple_of((seq * heads + h) * dim, dim), dim)],
                back_send.at[h], back_recv.at[h], (p, fs),
            )
            return carry

        lax.fori_loop(1, 16, body, 0)
        if PARTS["attend"]:
            for part in range(per):
                sent[h, seq, pl.ds(part * dim, dim), :] = attend(h, seq * per + part)
        pltpu.make_async_copy(
            sent.at[h, seq], rows.at[:, pl.ds(pl.multiple_of((seq * heads + h) * dim, dim), dim)],
            back_recv.at[h],
        ).start()

    if PARTS["a2a"]:
        for t, (hbm, buf) in enumerate(streams):
            scattered(buf, t, 0)
        attend_head(0)
    if PARTS["gather"]:
        relay_blocks(1)
        last_blocks(1)
        finish_blocks(0)
    if PARTS["a2a"]:
        for t, (hbm, buf) in enumerate(streams):
            scattered(buf, t, 1)
        attend_head(1)
    if PARTS["gather"]:
        finish_blocks(1)

    if PARTS["gather"]:
        for p in range(2):
            for n, (which, j) in enumerate((
                (p, fs), (p, down), (p, up), (1 - p, far + y), (p, opp),
                (1 - p, far + (y + 3) % 4), (1 - p, far + (y + 1) % 4), (1 - p, far + (y + 2) % 4),
            )):
                view = wb.at[xl if which == 0 else 1 - xl, :, 1 - c, j]
                arrived(view, sib_recv.at[p * 8 + n])
        for copy in pending:
            copy.wait_send()
    if PARTS["a2a"]:
        for h in range(heads):
            arrived(rows.at[:, pl.ds(0, 16 * dim)], back_recv.at[h])
            arrived(sent.at[h, pl.ds(0, 15)], back_send.at[h])
            for t, (hbm, buf) in enumerate(streams):
                arrived(buf[h].at[pl.ds(0, 15 * per)], out_sems.at[t, h])

    chunk = 256
    if PARTS["project"]:
        def project(n, carry):
            cols = pl.ds(pl.multiple_of(n * chunk, chunk), chunk)
            w = wb[:, :, :, :, :, cols].reshape(-1, chunk)
            outv[:, cols] = jnp.dot(rows[...], w, preferred_element_type=jnp.float32).astype(jnp.bfloat16)
            return carry

        lax.fori_loop(0, outv.shape[1] // chunk, project, 0)
    done = pltpu.make_async_copy(outv, out_hbm.at[0], own_sem.at[1])
    done.start()
    done.wait()


def shards(queries, keys, values, out_weight, block_lists, block_counts):
    seq = lax.axis_index("seq")
    groups = lax.axis_size("seq")
    others = lax.axis_size("fsdp")
    head_count = block_counts.shape[1]
    blocks = block_counts.shape[2]
    heads = head_count // groups
    span = queries.shape[1]
    dim = queries.shape[2] // head_count
    depth, width = out_weight.shape
    block = span * groups // blocks
    lists = lax.dynamic_slice_in_dim(block_lists[0], seq * heads, heads).reshape(-1)
    counts = lax.dynamic_slice_in_dim(block_counts[0], seq * heads, heads).reshape(-1)
    bf16 = jnp.bfloat16
    dma = pltpu.SemaphoreType.DMA
    hbm = pl.BlockSpec(memory_space=pl.ANY)
    smem = pl.BlockSpec(memory_space=pltpu.SMEM)
    head_buf = pltpu.VMEM((blocks, block, dim), bf16)
    return pl.pallas_call(
        kernel,
        out_shape=jax.ShapeDtypeStruct((1, span, width), bf16),
        in_specs=[smem, smem, hbm, hbm, hbm, hbm],
        out_specs=hbm,
        scratch_shapes=[
            *[head_buf] * (3 * heads),
            pltpu.VMEM((heads, groups, span, dim), bf16),
            pltpu.VMEM((span, head_count * dim), bf16),
            pltpu.VMEM((2, 4, 2, others, depth, width), bf16),
            pltpu.VMEM((span, width), bf16),
            dma((3, heads)), dma((3, heads)), dma((2,)),
            dma((18,)), dma((21,)), dma((16,)), dma((16,)),
            dma((heads,)), dma((heads,)),
        ],
        compiler_params=pltpu.CompilerParams(
            collective_id=0, has_side_effects=True, vmem_limit_bytes=60 << 20,
        ),
    )(lists, counts, queries, keys, values, out_weight)


def solution(mesh):
    return jax.shard_map(
        shards,
        mesh=mesh,
        in_specs=(
            P("fsdp", "seq", None),
            P("fsdp", "seq", None),
            P("fsdp", "seq", None),
            P(("seq", "fsdp"), None),
            P("fsdp", None, None, None),
            P("fsdp", None, None),
        ),
        out_specs=P("fsdp", "seq", None),
        check_vma=False,
    )
```

time: 445 us -> 154 us (0.35); the launches traced: 440 us -> 154 us
  waiting for transfers between devices: 157 us -> 0 us
  Pallas kernels: 0 us -> 149 us
  blocking collectives: 87.6 us -> 0 us
  local copies, waits for them, and re-layouts: 76 us -> 4.8 us
  matrix products: 69.4 us -> 0 us
  starting transfers between devices: 17.3 us -> 0 us
  between operations: 13.5 us -> 0.01 us
  other arithmetic: 11.5 us -> 0 us
  loops' own time: 7.99 us -> 0 us
    pallas_call x0 -> x1, Pallas kernels: none -> 149 us  [shards(): pl.pallas_call(kernel, out_shape=jax.ShapeDtypeStruct((1, span, width), b...]
    all_to_all x1 -> x0, blocking collectives: 87.6 us -> none  [shards(): lax.all_to_all(attended, 'seq', split_axis=0, concat_axis=1, tiled=True)]
    all_to_all x3 -> x0, waiting for transfers between devices: 84.9 us -> none  [the longest x1 30 us: shards(): lax.all_to_all(local_value, 'seq', split_axis=1, concat_axis=0, tiled=True)]
    all_gather x1 -> x0, waiting for transfers between devices: 71.2 us -> none  [shards(): lax.all_gather(out_weight, ('seq', 'fsdp'), axis=0, tiled=True)]
    dot_general x21 -> x0, matrix products: 69.4 us -> none  [the longest x10 35.6 us: advance(): jnp.einsum('qpk,qkd->qpd', weights.astype(jnp.bfloat16), value_tile, pref...]
    gather x22 -> x0, local copies, waits for them, and re-layouts: 40.7 us -> none  [the longest x10 19.8 us: advance(): key_tile = key_blocks[picked]]
    all_to_all x3 -> x0, starting transfers between devices: 17.3 us -> none  [the longest x1 7.76 us: shards(): lax.all_to_all(local_key, 'seq', split_axis=1, concat_axis=0, tiled=True)]
    all_to_all x4 -> x0, local copies, waits for them, and re-layouts: 13.1 us -> none  [the longest x1 3.92 us: shards(): lax.all_to_all(local_query, 'seq', split_axis=1, concat_axis=0, tiled=True)]
  transfers between devices with their start and end apart: 4 -> 0, of which waited for: 4 -> 0; matrix products, arithmetic and copies ran while one was open for 33% -> 0% of each run, Pallas kernels for 0% -> 0%
where the time goes in v1:
time: 154 us
  Pallas kernels  149 us (97%)
  local copies, waits for them, and re-layouts  4.8 us (3%)
    pallas_call x1, Pallas kernels, shards(): pl.pallas_call(kernel, out_shape=jax.ShapeDtypeStruct((1, span, width), b...  149 us

profile of v1, /device:TPU:1, one launch (start us, length us, event | category | flops | bytes accessed | tf_op | source)
XLA Modules:
  0.0 153.6 jit_solution(1517421251410412395)
XLA Ops:
  0.0 0.0 copy-start
  0.0 0.7 constant_dynamic-slice_fusion
  0.7 0.7 reshape.11.counts
  1.4 0.0 copy-done
  1.4 0.1 copy.7
  1.5 0.7 reshape.10.lists
  2.2 148.8 %shard_map.64 = bf16[1,256,3072]{2,1,0:T(8,128)(2,1)} custom-call(s32[512]{0:T(512)} %reshape.10.lists, s32[64]{0:T(128)} %reshape.11.counts, bf16[1,256,4096]{2,1,0:T(8,128)(2,1)} %q_hbm.1, bf16[1,256,4096]{2,1,0:T(8,128)(2,1)} %k_hbm.1, bf16[1,256,4096]{2,1,0:T(8,128)(2,1)} %v_hbm.1, bf16[32,3072]{1,0:T(8,128)(2,1)} %w_hbm.1), custom_call_target="tpu_custom_call" | custom-call | tf_op jit(solution)/shard_map/pallas_call | solution.py:277
  150.9 2.7 %copy.9 = bf16[1,256,3072]{2,1,0:T(8,128)(2,1)} copy(bf16[1,256,3072]{2,1,0:T(8,128)(2,1)} %shard_map.64) | data formatting | bytes 3145728
  (1 shorter events, 0.0 us)
Async XLA Ops:
  0.0 1.4 copy-start

commit v2 on v0

v2 whole, which is shorter than its diff:
```python
import functools
import math

import jax
import jax.numpy as jnp
from jax import lax
from jax.experimental import pallas as pl
from jax.experimental.pallas import tpu as pltpu
from jax.sharding import PartitionSpec as P

MESH = pl.DeviceIdType.MESH
GROUP = 4
BOTH = (3,)
PARTS = dict(a2a=True, gather=True, attend=True, project=True)


def kernel(
    lists_hbm, counts_hbm, q_hbm, k_hbm, v_hbm, w_hbm, out_hbm,
    lists, counts, q0, q1, k0, k1, v0, v1, sent, rows, wb, acc, outv,
    in_sems, q_sems, out_sems, own_sem, w_recv, w_send, sib_recv, sib_send,
    back_recv, back_send,
):
    seq = lax.axis_index("seq")
    fs = lax.axis_index("fsdp")
    xl, z, c = seq // 8, (seq // 2) % 4, seq % 2
    xh, y = fs // 4, fs % 4
    qb, kb, vb = (q0, q1), (k0, k1), (v0, v1)
    heads, blocks, dim = len(qb), q0.shape[0], q0.shape[2]
    per = q_hbm.shape[0]
    span = per * dim

    def seq_of(a, b, d):
        return (a * 4 + b) * 2 + d

    up, down = xh * 4 + (y + 1) % 4, xh * 4 + (y + 3) % 4
    opp = xh * 4 + (y + 2) % 4
    far = (1 - xh) * 4
    x_peer = (seq_of(1 - xl, z, c), fs)
    far_peer = (seq_of(1 - xl, z, c), far + y)
    sibling = (seq_of(xl, z, 1 - c), fs)
    z_up, z_down = (z + 1) % 4, (z + 3) % 4
    z_opp = (z + 2) % 4
    up_peer, down_peer = (seq, up), (seq, down)

    barrier = pltpu.get_barrier_semaphore()
    for d in range(1, 16):
        pl.semaphore_signal(barrier, inc=1, device_id=((seq + d) % 16, fs), device_id_type=MESH)
    for peer in (far_peer, up_peer, down_peer):
        pl.semaphore_signal(barrier, inc=1, device_id=peer, device_id_type=MESH)
    fetched = [
        pltpu.make_async_copy(lists_hbm.at[0, pl.ds(seq * heads, heads)], lists, own_sem.at[2]),
        pltpu.make_async_copy(counts_hbm.at[0], counts, own_sem.at[3]),
    ]
    own = wb.at[xl, z, c, fs]
    if PARTS["gather"]:
        fetched.append(pltpu.make_async_copy(w_hbm, own, own_sem.at[0]))
    for copy in fetched:
        copy.start()
    for h in range(heads):
        vb[h][:blocks, :, dim:] = jnp.ones((blocks, dim, dim), jnp.bfloat16)
        vb[h][blocks] = jnp.zeros((dim, 2 * dim), jnp.bfloat16)
    for copy in fetched:
        copy.wait()
    pl.semaphore_wait(barrier, 18)

    pending = []

    def send(src, dst, ssem, rsem, peer):
        copy = pltpu.make_async_remote_copy(
            src_ref=src, dst_ref=dst, send_sem=ssem, recv_sem=rsem,
            device_id=peer, device_id_type=MESH,
        )
        copy.start()
        return copy

    def share(view, n, peer):
        pending.append(send(view, view, w_send.at[n], w_recv.at[n], peer))

    def arrived(ref, sem):
        pltpu.make_async_copy(ref, ref, sem).wait()

    def landing(buf, first, count):
        view = buf.at[pl.ds(first, count)]
        return view if buf.shape[2] == dim else view.at[:, :, pl.ds(0, dim)]

    order = [(dx, dz, dc) for dz in (2, 1, 3, 0) for dx in (1, 0) for dc in (1, 0)]

    def peer_at(n, way):
        dx, dz, dc = order[n]
        return seq_of((xl + dx) % 2, (z + 4 + way * dz) % 4, (c + dc) % 2)

    def scatter(hbm, buf, h, out_sem, in_sem):
        if not PARTS["a2a"]:
            return
        mine = landing(buf[h], seq * per, per)
        for n in range(16):
            p = peer_at(n, 1)
            block = hbm.at[:, :, pl.ds(pl.multiple_of((p * heads + h) * dim, dim), dim)]
            if n < 15:
                send(block, mine, out_sem, in_sem(n), (p, fs))
            else:
                pltpu.make_async_copy(block, mine, in_sem(n)).start()

    def scatter_k(h):
        scatter(k_hbm, kb, h, out_sems.at[0, h], lambda n: in_sems.at[0, h])

    def scatter_v(h):
        scatter(v_hbm, vb, h, out_sems.at[1, h], lambda n: in_sems.at[1, h])

    def scatter_q(h):
        scatter(q_hbm, qb, h, out_sems.at[2, h], lambda n: q_sems.at[h, n // GROUP])

    def scattered(h):
        if PARTS["a2a"]:
            arrived(landing(kb[h], 0, blocks), in_sems.at[0, h])
            arrived(landing(vb[h], 0, blocks), in_sems.at[1, h])

    def queries_in(h, g):
        if PARTS["a2a"]:
            arrived(qb[h].at[pl.ds(0, GROUP * per)], q_sems.at[h, g])

    def pair(d, j):
        return wb.at[:, (z + d) % 4, c, j]

    def to_sibling(d, kind, view):
        n = d * 8 + kind
        pending.append(send(view, view, sib_send.at[n], sib_recv.at[n], sibling))

    def slot(d, kind):
        return 8 + d * 10 + kind

    def blocks_out(d):
        view = pair(d, fs)
        if d > 0:
            for kind, peer in ((0, up_peer), (1, down_peer), (2, far_peer)):
                share(view, slot(d, kind), peer)
        to_sibling(d, 0, view)

    def arrived_pair(d, j, kind, flip):
        if d > 0:
            arrived(pair(d, j), w_recv.at[slot(d, kind)])
        else:
            first = 1 - xl if flip else xl
            arrived(wb.at[first, z, c, j], w_recv.at[5 + kind])
            arrived(wb.at[1 - first, z, c, j], w_recv.at[slot(0, kind)])

    def relay_y(d):
        below, above = pair(d, down), pair(d, up)
        arrived_pair(d, down, 0, False)
        share(below.at[0], slot(d, 3), up_peer)
        if d in BOTH:
            share(below.at[1], slot(d, 8), far_peer)
        to_sibling(d, 1, below)
        arrived_pair(d, up, 1, False)
        share(above.at[1], slot(d, 4), down_peer)
        if d in BOTH:
            share(above.at[0], slot(d, 9), far_peer)
        to_sibling(d, 2, above)

    def relay_far(d):
        across = pair(d, far + y)
        arrived_pair(d, far + y, 2, True)
        share(across.at[0] if d in BOTH else across, slot(d, 5), up_peer)
        share(across.at[1] if d in BOTH else across, slot(d, 6), down_peer)
        to_sibling(d, 3, across)

    def relay_opp(d):
        facing = pair(d, opp)
        arrived(facing.at[0], w_recv.at[slot(d, 3)])
        arrived(facing.at[1], w_recv.at[slot(d, 4)])
        share(facing, slot(d, 7), far_peer)
        to_sibling(d, 4, facing)

    def finish(d):
        low, high, last = (pair(d, far + (y + n) % 4) for n in (3, 1, 2))
        if d in BOTH:
            arrived(low.at[0], w_recv.at[slot(d, 5)])
            arrived(low.at[1], w_recv.at[slot(d, 8)])
            arrived(high.at[1], w_recv.at[slot(d, 6)])
            arrived(high.at[0], w_recv.at[slot(d, 9)])
        else:
            arrived(low, w_recv.at[slot(d, 5)])
            arrived(high, w_recv.at[slot(d, 6)])
        to_sibling(d, 5, low)
        to_sibling(d, 6, high)
        arrived(last, w_recv.at[slot(d, 7)])
        to_sibling(d, 7, last)

    def z_peer(zz):
        return (seq_of(xl, zz, c), fs)

    def gather_own():
        share(own, 0, x_peer)
        for kind, peer in ((0, up_peer), (1, down_peer), (2, far_peer)):
            share(own, 5 + kind, peer)

    def gather_x():
        other = wb.at[1 - xl, z, c, fs]
        arrived(other, w_recv.at[0])
        share(pair(0, fs), 1, z_peer(z_up))
        share(pair(0, fs), 2, z_peer(z_down))
        for kind, peer in ((0, up_peer), (1, down_peer), (2, far_peer)):
            share(other, slot(0, kind), peer)
        blocks_out(0)

    def gather_z():
        arrived(pair(3, fs), w_recv.at[1])
        share(wb.at[0, z_down, c, fs], 3, z_peer(z_up))
        arrived(pair(1, fs), w_recv.at[2])
        share(wb.at[1, z_up, c, fs], 4, z_peer(z_down))
        blocks_out(3)
        blocks_out(1)

    def gather_opp():
        arrived(wb.at[0, z_opp, c, fs], w_recv.at[3])
        arrived(wb.at[1, z_opp, c, fs], w_recv.at[4])
        blocks_out(2)

    def run(step, *args):
        if PARTS["gather"]:
            step(*args)

    scale = dim ** -0.5 * math.log2(math.e)

    def attend(h, i):
        live = counts[seq * heads + h, i]
        first = lists[h, i, 0]
        ids = [lists[h, i, j] for j in range(8)]
        key_ids = [jnp.where(j < live, ids[j], first) for j in range(8)]
        value_ids = [jnp.where(j < live, ids[j], blocks) for j in range(8)]
        q = qb[h][i]
        scores = []
        for j in range(0, 8, 2):
            keys = jnp.concatenate([kb[h][key_ids[j]], kb[h][key_ids[j + 1]]], axis=0)
            scores.append(lax.dot_general(q, keys, (((1,), (1,)), ((), ())), preferred_element_type=jnp.float32))
        top = jnp.maximum(jnp.maximum(scores[0], scores[1]), jnp.maximum(scores[2], scores[3]))
        top = jnp.max(jnp.maximum(top[:, :dim], top[:, dim:]), axis=1, keepdims=True)
        mixed = None
        for j in range(0, 8, 2):
            weights = jnp.exp2((scores[j // 2] - top) * scale).astype(jnp.bfloat16)
            values = jnp.concatenate([vb[h][value_ids[j]], vb[h][value_ids[j + 1]]], axis=0)
            part = jnp.dot(weights, values, preferred_element_type=jnp.float32)
            mixed = part if mixed is None else mixed + part
        return (mixed[:, :dim] / mixed[:, dim:]).astype(jnp.bfloat16)

    def attend_group(h, g):
        if not PARTS["a2a"]:
            return
        queries_in(h, g)
        peers = [peer_at(g * GROUP + n, -1) for n in range(GROUP)]
        if PARTS["attend"]:
            done = [[attend(h, p * per + part) for part in range(per)] for p in peers]
            for p, blocks_of in zip(peers, done):
                for part in range(per):
                    sent[h, p, pl.ds(part * dim, dim), :] = blocks_of[part]
        columns = pl.ds(pl.multiple_of((h * 16 + seq) * dim, dim), dim)
        for n, p in enumerate(peers):
            if g * GROUP + n < 15:
                send(sent.at[h, p], rows.at[:, columns], back_send.at[h], back_recv.at[h], (p, fs))
            else:
                pltpu.make_async_copy(sent.at[h, p], rows.at[:, columns], back_recv.at[h]).start()

    def returned(h):
        if PARTS["a2a"]:
            arrived(rows.at[:, pl.ds(h * 16 * dim, 16 * dim)], back_recv.at[h])

    def from_sibling():
        for d in range(4):
            for kind, j in enumerate((
                fs, down, up, far + y, opp, far + (y + 3) % 4, far + (y + 1) % 4, far + (y + 2) % 4,
            )):
                arrived(wb.at[:, (z + d) % 4, 1 - c, j], sib_recv.at[d * 8 + kind])

    chunk = 256
    others, depth = wb.shape[3], wb.shape[4]

    def project(h, last):
        if not PARTS["project"]:
            return
        lower = h * dim // depth
        near = pl.ds(lower, dim // depth)

        def body(n, carry):
            cols = pl.ds(pl.multiple_of(n * chunk, chunk), chunk)
            w = wb[:, :, :, near, :, cols].reshape(16 * dim, chunk)
            part = jnp.dot(rows[:, h * 16 * dim:(h + 1) * 16 * dim], w, preferred_element_type=jnp.float32)
            if h > 0:
                part = acc[:, cols] + part
            if last:
                outv[:, cols] = part.astype(jnp.bfloat16)
                pltpu.make_async_copy(outv.at[:, cols], out_hbm.at[0, :, cols], own_sem.at[1]).start()
            else:
                acc[:, cols] = part
            return carry

        lax.fori_loop(0, outv.shape[1] // chunk, body, 0)

    run(gather_own)
    run(gather_x)
    run(gather_z)
    scatter_k(0)
    run(gather_opp)
    scatter_v(0)
    scatter_q(0)
    run(relay_y, 0)
    run(relay_far, 0)
    scatter_k(1)
    scatter_v(1)
    scatter_q(1)
    run(relay_y, 3)
    run(relay_far, 3)
    run(relay_y, 1)
    run(relay_far, 1)
    run(relay_y, 2)
    run(relay_far, 2)
    run(relay_opp, 0)
    scattered(0)
    attend_group(0, 0)
    run(relay_opp, 3)
    attend_group(0, 1)
    run(relay_opp, 1)
    attend_group(0, 2)
    run(relay_opp, 2)
    attend_group(0, 3)
    run(finish, 0)
    run(finish, 3)
    scattered(1)
    attend_group(1, 0)
    attend_group(1, 1)
    attend_group(1, 2)
    attend_group(1, 3)
    run(finish, 1)
    run(finish, 2)
    run(from_sibling)
    returned(0)
    project(0, False)
    returned(1)
    project(1, True)
    if PARTS["gather"]:
        for copy in pending:
            copy.wait_send()
    if PARTS["a2a"]:
        for h in range(heads):
            arrived(sent.at[h, pl.ds(0, 15)], back_send.at[h])
            for t in range(3):
                arrived(qb[h].at[pl.ds(0, 15 * per)], out_sems.at[t, h])
    if PARTS["project"]:
        arrived(outv, own_sem.at[1])


def shards(queries, keys, values, out_weight, block_lists, block_counts):
    groups = lax.axis_size("seq")
    others = lax.axis_size("fsdp")
    head_count = block_counts.shape[1]
    blocks = block_counts.shape[2]
    heads = head_count // groups
    span = queries.shape[1]
    dim = queries.shape[2] // head_count
    depth, width = out_weight.shape
    block = span * groups // blocks
    bf16 = jnp.bfloat16
    dma = pltpu.SemaphoreType.DMA
    hbm = pl.BlockSpec(memory_space=pl.ANY)
    head_buf = pltpu.VMEM((blocks, block, dim), bf16)
    return pl.pallas_call(
        kernel,
        out_shape=jax.ShapeDtypeStruct((1, span, width), bf16),
        in_specs=[hbm] * 6,
        out_specs=hbm,
        scratch_shapes=[
            pltpu.SMEM((heads, blocks, block_lists.shape[3]), jnp.int32),
            pltpu.SMEM((head_count, blocks), jnp.int32),
            *[head_buf] * (2 * heads),
            *[pltpu.VMEM((blocks + 1, block, 2 * dim), bf16)] * heads,
            pltpu.VMEM((heads, groups, span, dim), bf16),
            pltpu.VMEM((span, head_count * dim), bf16),
            pltpu.VMEM((2, 4, 2, others, depth, width), bf16),
            pltpu.VMEM((span, width), jnp.float32),
            pltpu.VMEM((span, width), bf16),
            dma((2, heads)), dma((heads, groups // GROUP)), dma((3, heads)), dma((4,)),
            dma((48,)), dma((48,)), dma((32,)), dma((32,)),
            dma((heads,)), dma((heads,)),
        ],
        compiler_params=pltpu.CompilerParams(
            collective_id=0, has_side_effects=True, vmem_limit_bytes=60 << 20,
        ),
    )(block_lists, block_counts, *(a.reshape(-1, block, a.shape[2]) for a in (queries, keys, values)), out_weight)


def solution(mesh):
    return jax.shard_map(
        shards,
        mesh=mesh,
        in_specs=(
            P("fsdp", "seq", None),
            P("fsdp", "seq", None),
            P("fsdp", "seq", None),
            P(("seq", "fsdp"), None),
            P("fsdp", None, None, None),
            P("fsdp", None, None),
        ),
        out_specs=P("fsdp", "seq", None),
        check_vma=False,
    )
```

time: 445 us -> 133 us (0.30)
  waiting for transfers between devices: 157 us -> 0 us
  Pallas kernels: 0 us -> 126 us
  blocking collectives: 87.6 us -> 0 us
  local copies, waits for them, and re-layouts: 76 us -> 4.57 us
  matrix products: 69.4 us -> 0 us
  starting transfers between devices: 17.3 us -> 0 us
  between operations: 13.5 us -> 0.01 us
  other arithmetic: 11.5 us -> 0 us
  loops' own time: 7.99 us -> 0 us
    pallas_call x0 -> x1, Pallas kernels: none -> 126 us  [shards(): pl.pallas_call(kernel, out_shape=jax.ShapeDtypeStruct((1, span, width), b...]
    all_to_all x1 -> x0, blocking collectives: 87.6 us -> none  [shards(): lax.all_to_all(attended, 'seq', split_axis=0, concat_axis=1, tiled=True)]
    all_to_all x3 -> x0, waiting for transfers between devices: 84.9 us -> none  [the longest x1 30 us: shards(): lax.all_to_all(local_value, 'seq', split_axis=1, concat_axis=0, tiled=True)]
    all_gather x1 -> x0, waiting for transfers between devices: 71.2 us -> none  [shards(): lax.all_gather(out_weight, ('seq', 'fsdp'), axis=0, tiled=True)]
    dot_general x21 -> x0, matrix products: 69.4 us -> none  [the longest x10 35.6 us: advance(): jnp.einsum('qpk,qkd->qpd', weights.astype(jnp.bfloat16), value_tile, pref...]
    gather x22 -> x0, local copies, waits for them, and re-layouts: 40.7 us -> none  [the longest x10 19.8 us: advance(): key_tile = key_blocks[picked]]
    all_to_all x3 -> x0, starting transfers between devices: 17.3 us -> none  [the longest x1 7.76 us: shards(): lax.all_to_all(local_key, 'seq', split_axis=1, concat_axis=0, tiled=True)]
    all_to_all x4 -> x0, local copies, waits for them, and re-layouts: 13.1 us -> none  [the longest x1 3.92 us: shards(): lax.all_to_all(local_query, 'seq', split_axis=1, concat_axis=0, tiled=True)]
  transfers between devices with their start and end apart: 4 -> 0, of which waited for: 4 -> 0; matrix products, arithmetic and copies ran while one was open for 33% -> 0% of each run, Pallas kernels for 0% -> 0%
where the time goes in v2:
time: 133 us; the launch traced here: 131 us
  Pallas kernels  126 us (95%)
  local copies, waits for them, and re-layouts  4.57 us (3%)
    pallas_call x1, Pallas kernels, shards(): pl.pallas_call(kernel, out_shape=jax.ShapeDtypeStruct((1, span, width), b...  126 us
    unnamed x2, local copies, waits for them, and re-layouts  4.57 us

profile of v2, /device:TPU:1, one launch (start us, length us, event | category | flops | bytes accessed | tf_op | source)
XLA Modules:
  0.0 131.0 jit_solution(12125003324665178085)
XLA Ops:
  0.0 1.9 %copy.7.lists_hbm = s32[1,32,32,8]{3,2,1,0:T(8,128)} copy(s32[1,32,32,8]{2,3,1,0:T(8,128)} %param.10) | data formatting | bytes 65536 | tf_op args[4]
  1.9 126.4 %shard_map.64 = bf16[1,256,3072]{2,1,0:T(8,128)(2,1)} custom-call(s32[1,32,32,8]{3,2,1,0:T(8,128)} %copy.7.lists_hbm, s32[1,32,32]{2,1,0:T(8,128)} %counts_hbm.1, bf16[2,128,4096]{2,1,0:T(8,128)(2,1)} %bitcast.3, bf16[2,128,4096]{2,1,0:T(8,128)(2,1)} %bitcast.4, bf16[2,128,4096]{2,1,0:T(8,128)(2,1)} %bitcast.5, bf16[32,3072]{1,0:T(8,128)(2,1)} %w_hbm.1), custom_call_target="tpu_custom_call" | custom-call | tf_op jit(solution)/shard_map/pallas_call | solution.py:365
  128.3 2.7 %copy.9 = bf16[1,256,3072]{2,1,0:T(8,128)(2,1)} copy(bf16[1,256,3072]{2,1,0:T(8,128)(2,1)} %shard_map.64) | data formatting | bytes 3145728

commit v3 on v2

--- a/solution.py
+++ b/solution.py
@@ -83,17 +83,17 @@
         view = buf.at[pl.ds(first, count)]
         return view if buf.shape[2] == dim else view.at[:, :, pl.ds(0, dim)]
 
-    order = [(dx, dz, dc) for dz in (2, 1, 3, 0) for dx in (1, 0) for dc in (1, 0)]
+    order = [(dx, dz, dc) for dc in (1, 0) for dx in (1, 0) for dz in (2, 1, 3, 0)]
 
     def peer_at(n, way):
         dx, dz, dc = order[n]
         return seq_of((xl + dx) % 2, (z + 4 + way * dz) % 4, (c + dc) % 2)
 
-    def scatter(hbm, buf, h, out_sem, in_sem):
+    def scatter(hbm, buf, h, out_sem, in_sem, lo, hi):
         if not PARTS["a2a"]:
             return
         mine = landing(buf[h], seq * per, per)
-        for n in range(16):
+        for n in range(lo, hi):
             p = peer_at(n, 1)
             block = hbm.at[:, :, pl.ds(pl.multiple_of((p * heads + h) * dim, dim), dim)]
             if n < 15:
@@ -101,14 +101,14 @@
             else:
                 pltpu.make_async_copy(block, mine, in_sem(n)).start()
 
-    def scatter_k(h):
-        scatter(k_hbm, kb, h, out_sems.at[0, h], lambda n: in_sems.at[0, h])
-
-    def scatter_v(h):
-        scatter(v_hbm, vb, h, out_sems.at[1, h], lambda n: in_sems.at[1, h])
-
-    def scatter_q(h):
-        scatter(q_hbm, qb, h, out_sems.at[2, h], lambda n: q_sems.at[h, n // GROUP])
+    def scatter_k(h, lo=0, hi=16):
+        scatter(k_hbm, kb, h, out_sems.at[0, h], lambda n: in_sems.at[0, h], lo, hi)
+
+    def scatter_v(h, lo=0, hi=16):
+        scatter(v_hbm, vb, h, out_sems.at[1, h], lambda n: in_sems.at[1, h], lo, hi)
+
+    def scatter_q(h, lo=0, hi=16):
+        scatter(q_hbm, qb, h, out_sems.at[2, h], lambda n: q_sems.at[h, n // GROUP], lo, hi)
 
     def scattered(h):
         if PARTS["a2a"]:
@@ -256,13 +256,14 @@
         columns = pl.ds(pl.multiple_of((h * 16 + seq) * dim, dim), dim)
         for n, p in enumerate(peers):
             if g * GROUP + n < 15:
-                send(sent.at[h, p], rows.at[:, columns], back_send.at[h], back_recv.at[h], (p, fs))
+                send(sent.at[h, p], rows.at[:, columns], back_send.at[h], back_recv.at[h, g], (p, fs))
             else:
-                pltpu.make_async_copy(sent.at[h, p], rows.at[:, columns], back_recv.at[h]).start()
-
-    def returned(h):
+                pltpu.make_async_copy(sent.at[h, p], rows.at[:, columns], back_recv.at[h, g]).start()
+
+    def returned(h, *groups):
         if PARTS["a2a"]:
-            arrived(rows.at[:, pl.ds(h * 16 * dim, 16 * dim)], back_recv.at[h])
+            for g in groups:
+                arrived(rows.at[:, pl.ds(0, GROUP * dim)], back_recv.at[h, g])
 
     def from_sibling():
         for d in range(4):
@@ -271,20 +272,21 @@
             )):
                 arrived(wb.at[:, (z + d) % 4, 1 - c, j], sib_recv.at[d * 8 + kind])
 
-    chunk = 256
+    chunk = 1024
     others, depth = wb.shape[3], wb.shape[4]
 
-    def project(h, last):
+    def project(h, first, last):
         if not PARTS["project"]:
             return
-        lower = h * dim // depth
-        near = pl.ds(lower, dim // depth)
+        near = pl.ds(h * dim // depth, dim // depth)
 
         def body(n, carry):
             cols = pl.ds(pl.multiple_of(n * chunk, chunk), chunk)
-            w = wb[:, :, :, near, :, cols].reshape(16 * dim, chunk)
-            part = jnp.dot(rows[:, h * 16 * dim:(h + 1) * 16 * dim], w, preferred_element_type=jnp.float32)
-            if h > 0:
+            part = jnp.dot(
+                rows[:, h * 16 * dim:(h + 1) * 16 * dim],
+                wb[:, :, :, near, :, cols].reshape(16 * dim, chunk), preferred_element_type=jnp.float32,
+            )
+            if not first:
                 part = acc[:, cols] + part
             if last:
                 outv[:, cols] = part.astype(jnp.bfloat16)
@@ -296,17 +298,16 @@
         lax.fori_loop(0, outv.shape[1] // chunk, body, 0)
 
     run(gather_own)
+    scatter_k(0)
     run(gather_x)
+    scatter_v(0)
     run(gather_z)
-    scatter_k(0)
+    scatter_q(0)
     run(gather_opp)
-    scatter_v(0)
-    scatter_q(0)
     run(relay_y, 0)
     run(relay_far, 0)
     scatter_k(1)
     scatter_v(1)
-    scatter_q(1)
     run(relay_y, 3)
     run(relay_far, 3)
     run(relay_y, 1)
@@ -317,25 +318,26 @@
     scattered(0)
     attend_group(0, 0)
     run(relay_opp, 3)
+    scatter_q(1)
     attend_group(0, 1)
     run(relay_opp, 1)
     attend_group(0, 2)
     run(relay_opp, 2)
     attend_group(0, 3)
-    run(finish, 0)
-    run(finish, 3)
     scattered(1)
     attend_group(1, 0)
+    run(finish, 0)
     attend_group(1, 1)
+    run(finish, 3)
     attend_group(1, 2)
+    run(finish, 1)
     attend_group(1, 3)
-    run(finish, 1)
     run(finish, 2)
     run(from_sibling)
-    returned(0)
-    project(0, False)
-    returned(1)
-    project(1, True)
+    returned(0, 0, 1, 2, 3)
+    project(0, True, False)
+    returned(1, 0, 1, 2, 3)
+    project(1, False, True)
     if PARTS["gather"]:
         for copy in pending:
             copy.wait_send()
@@ -379,7 +381,7 @@
             pltpu.VMEM((span, width), bf16),
             dma((2, heads)), dma((heads, groups // GROUP)), dma((3, heads)), dma((4,)),
             dma((48,)), dma((48,)), dma((32,)), dma((32,)),
-            dma((heads,)), dma((heads,)),
+            dma((heads, groups // GROUP)), dma((heads,)),
         ],
         compiler_params=pltpu.CompilerParams(
             collective_id=0, has_side_effects=True, vmem_limit_bytes=60 << 20,

time: 133 us -> 129 us (0.970); the launches traced: 131 us -> 128 us
  Pallas kernels: 126 us -> 124 us
    pallas_call x1, Pallas kernels: 126 us -> 124 us  [shards(): pl.pallas_call(kernel, out_shape=jax.ShapeDtypeStruct((1, span, width), b...]
where the time goes in v3:
time: 129 us; the launch traced here: 128 us
  Pallas kernels  124 us (96%)
  local copies, waits for them, and re-layouts  4.57 us (4%)
    pallas_call x1, Pallas kernels, shards(): pl.pallas_call(kernel, out_shape=jax.ShapeDtypeStruct((1, span, width), b...  124 us
    unnamed x2, local copies, waits for them, and re-layouts  4.57 us

profile of v3, /device:TPU:1, one launch (start us, length us, event | category | flops | bytes accessed | tf_op | source)
XLA Modules:
  0.0 128.3 jit_solution(2208030189988931576)
XLA Ops:
  0.0 1.9 %copy.7.lists_hbm = s32[1,32,32,8]{3,2,1,0:T(8,128)} copy(s32[1,32,32,8]{2,3,1,0:T(8,128)} %param.10) | data formatting | bytes 65536 | tf_op args[4]
  1.9 123.8 %shard_map.64 = bf16[1,256,3072]{2,1,0:T(8,128)(2,1)} custom-call(s32[1,32,32,8]{3,2,1,0:T(8,128)} %copy.7.lists_hbm, s32[1,32,32]{2,1,0:T(8,128)} %counts_hbm.1, bf16[2,128,4096]{2,1,0:T(8,128)(2,1)} %bitcast.3, bf16[2,128,4096]{2,1,0:T(8,128)(2,1)} %bitcast.4, bf16[2,128,4096]{2,1,0:T(8,128)(2,1)} %bitcast.5, bf16[32,3072]{1,0:T(8,128)(2,1)} %w_hbm.1), custom_call_target="tpu_custom_call" | custom-call | tf_op jit(solution)/shard_map/pallas_call | solution.py:367
  125.7 2.7 %copy.9 = bf16[1,256,3072]{2,1,0:T(8,128)(2,1)} copy(bf16[1,256,3072]{2,1,0:T(8,128)(2,1)} %shard_map.64) | data formatting | bytes 3145728

commit v4 on v3

--- a/solution.py
+++ b/solution.py
@@ -300,10 +300,11 @@
     run(gather_own)
     scatter_k(0)
     run(gather_x)
-    scatter_v(0)
+    scatter_v(0, 0, 8)
     run(gather_z)
+    scatter_v(0, 8, 16)
+    run(gather_opp)
     scatter_q(0)
-    run(gather_opp)
     run(relay_y, 0)
     run(relay_far, 0)
     scatter_k(1)

time: 129 us -> 126 us (0.977)
  Pallas kernels: 124 us -> 122 us
    pallas_call x1, Pallas kernels: 124 us -> 122 us  [shards(): pl.pallas_call(kernel, out_shape=jax.ShapeDtypeStruct((1, span, width), b...]
where the time goes in v4:
time: 126 us
  Pallas kernels  122 us (97%)
  local copies, waits for them, and re-layouts  4.57 us (4%)
    pallas_call x1, Pallas kernels, shards(): pl.pallas_call(kernel, out_shape=jax.ShapeDtypeStruct((1, span, width), b...  122 us
    unnamed x2, local copies, waits for them, and re-layouts  4.57 us

profile of v4, /device:TPU:1, one launch (start us, length us, event | category | flops | bytes accessed | tf_op | source)
XLA Modules:
  0.0 126.1 jit_solution(7042222277701003000)
XLA Ops:
  0.0 1.9 %copy.7.lists_hbm = s32[1,32,32,8]{3,2,1,0:T(8,128)} copy(s32[1,32,32,8]{2,3,1,0:T(8,128)} %param.10) | data formatting | bytes 65536 | tf_op args[4]
  1.9 121.5 %shard_map.64 = bf16[1,256,3072]{2,1,0:T(8,128)(2,1)} custom-call(s32[1,32,32,8]{3,2,1,0:T(8,128)} %copy.7.lists_hbm, s32[1,32,32]{2,1,0:T(8,128)} %counts_hbm.1, bf16[2,128,4096]{2,1,0:T(8,128)(2,1)} %bitcast.3, bf16[2,128,4096]{2,1,0:T(8,128)(2,1)} %bitcast.4, bf16[2,128,4096]{2,1,0:T(8,128)(2,1)} %bitcast.5, bf16[32,3072]{1,0:T(8,128)(2,1)} %w_hbm.1), custom_call_target="tpu_custom_call" | custom-call | tf_op jit(solution)/shard_map/pallas_call | solution.py:368
  123.4 2.7 %copy.9 = bf16[1,256,3072]{2,1,0:T(8,128)(2,1)} copy(bf16[1,256,3072]{2,1,0:T(8,128)(2,1)} %shard_map.64) | data formatting | bytes 3145728
